TPU v7x, 256 devices: a whole 4x4x8 slice. The times are simulated.
256 devices in a mesh: batch: 4 (over z_lo, core), row: 4 (over x), col: 16 (over y, z_hi).
Axes of the slice: x: 4, y: 4, z: 8 (z_hi: 4, z_lo: 2; z = z_hi * 2 + z_lo), core: 2. Of those that a mesh axis runs over, the one named last changes fastest.
Arguments:
- embeddings: bfloat16 [512, 128, 512], P('batch', 'col', 'row'), may hold values from -170 to 170
- projection: bfloat16 [512, 32], replicated, may hold values from -0.25 to 0.25
- w_in: bfloat16 [16384, 2048], P('row', 'col'), may hold values from -0.046875 to 0.046875
- bias: float32 [2048], P('col'), may hold values from -3 to 3
- w_out: bfloat16 [2048, 128, 512], P(None, 'col', 'row'), may hold values from -0.125 to 0.125
- cotangent: bfloat16 [512, 128, 512], P('batch', 'col', 'row'), may hold values from -0.1796875 to 0.1796875
Outputs:
- mixed: bfloat16 [512, 128, 512], P('batch', 'col', 'row')
- grad_out: float32 [2048, 128, 512], P('batch', 'col', 'row')
- grad_in: float32 [16384, 2048], P('row', 'col')
- grad_bias: float32 [2048], P('col')
- grad_proj: float32 [512, 32], P('row')
All inputs are finite; a program needn't handle non-finite values.
Results may differ from a plain program's by a relative error of at most 0.006.
Values may be sent and summed in bfloat16 or wider, within the bound.
A program may use at most 128 MiB of HBM per device.

v0:
```python
import jax
import jax.numpy as jnp
from jax import lax
from jax.sharding import PartitionSpec as P

epsilon = 1e-06


def copy_for_each(array, axis):
    size = lax.axis_size(axis)
    return lax.all_to_all(
        jnp.broadcast_to(array[None], (size, *array.shape)), axis, 0, 0, tiled=True
    )


def of_everyone(array, axis):
    everything = copy_for_each(array, axis)
    return jnp.sum(everything, axis=0)


def joined_along(tiles, dim):
    tiles = jnp.moveaxis(tiles, 0, dim)
    lengths = tiles.shape
    return tiles.reshape(*lengths[:dim], lengths[dim] * lengths[dim + 1], *lengths[dim + 2 :])


def gathered_copies(array, axis, dim):
    return joined_along(copy_for_each(array, axis), dim)


def cut_along(array, dim, size):
    lengths = array.shape
    tiles = array.reshape(*lengths[:dim], size, lengths[dim] // size, *lengths[dim + 1 :])
    return jnp.moveaxis(tiles, dim, 0)


def sent_and_summed(array, axis, dim):
    size = lax.axis_size(axis)
    tiles = lax.all_to_all(cut_along(array, dim, size), axis, 0, 0, tiled=True)
    return jnp.sum(tiles, axis=0)


def in_one_piece(arrays, axis, dim, along):
    both = jnp.concatenate(arrays, axis=along)
    whole, at, gathered = (lax.all_gather(both, axis, axis=dim, tiled=True), 0, [])
    for a in arrays:
        gathered.append(lax.slice_in_dim(whole, at, at + a.shape[along], axis=along))
        at += a.shape[along]
    return tuple(gathered)


def filled_up(lines, size):
    spare = -lines.shape[0] % size
    if not spare:
        return lines
    return jnp.concatenate([lines, jnp.zeros((spare, *lines.shape[1:]), lines.dtype)])


def sum_by_parts(array, axis):
    lines = array.reshape(-1, *array.shape[1:][-1:])
    padded = filled_up(lines, lax.axis_size(axis))
    own = lax.psum_scatter(padded, axis, scatter_dimension=0, tiled=True)
    whole = lax.all_gather(own, axis, axis=0, tiled=True)
    return whole[: len(lines)].reshape(array.shape)


def contract_first(left, right):
    return lax.dot_general(
        left, right, (((0,), (0,)), ((), ())), preferred_element_type=jnp.float32
    )


def contract_last(left, right):
    return lax.dot_general(
        left, right, (((1,), (1,)), ((), ())), preferred_element_type=jnp.float32
    )


def local(embeddings, projection, w_in, bias, w_out, cotangent):
    highest = lax.Precision.HIGHEST
    tok_rows, feat_local, emb_local = embeddings.shape
    rank_cols = projection.shape[1]
    row_count = lax.axis_size("row")
    row_place = lax.axis_index("row")
    emb_float = embeddings.astype(jnp.float32)
    own_proj = lax.dynamic_slice_in_dim(projection, row_place * emb_local, emb_local, 0)
    folded = of_everyone(
        jnp.einsum("bde,ek->bdk", embeddings, own_proj, preferred_element_type=jnp.float32), "row"
    )
    partial_value = jnp.einsum("bde,bdk->bek", emb_float, folded, precision=highest)
    interact = lax.psum(partial_value, "col")
    feature_count = emb_local * row_count * rank_cols
    square_sum = of_everyone(jnp.sum(interact * interact, axis=(1, 2)), "row")
    inv_rms = lax.rsqrt(square_sum / feature_count + epsilon)[:, None, None]
    normed = interact * inv_rms
    activated = normed.astype(jnp.bfloat16).reshape(tok_rows, emb_local * rank_cols)
    preact = of_everyone(jnp.dot(activated, w_in, preferred_element_type=jnp.float32), "row") + bias
    hidden = jax.nn.silu(preact).astype(jnp.bfloat16)
    hidden_all = gathered_copies(hidden, "col", 1)
    flat_out = w_out.reshape(w_out.shape[0], feat_local * emb_local)
    mixed = (
        jnp.dot(hidden_all, flat_out, preferred_element_type=jnp.float32)
        .astype(jnp.bfloat16)
        .reshape(tok_rows, feat_local, emb_local)
    )
    cot_rows = cotangent.reshape(tok_rows, feat_local * emb_local)
    d_cols = sent_and_summed(contract_last(cot_rows, flat_out), "col", 1)
    d_hidden = of_everyone(d_cols, "row")
    sigmoid_pre = jax.nn.sigmoid(preact)
    d_preact = d_hidden * sigmoid_pre * (1.0 + preact * (1.0 - sigmoid_pre))
    d_pre_b = d_preact.astype(jnp.bfloat16)
    per_batch = w_out.shape[0] // lax.axis_size("batch")
    every_hidden, every_cot = in_one_piece((hidden_all, cot_rows), "batch", 0, 1)
    own_hidden = lax.dynamic_slice_in_dim(
        every_hidden, lax.axis_index("batch") * per_batch, per_batch, 1
    )
    grad_flat = contract_first(own_hidden, every_cot)
    grad_out = grad_flat.reshape(per_batch, feat_local, emb_local)
    grad_in, grad_bias = lax.psum(
        (contract_first(activated, d_pre_b), jnp.sum(d_preact, axis=0)), "batch"
    )
    d_act = sum_by_parts(contract_last(d_pre_b, w_in), "col").reshape(
        tok_rows, emb_local, rank_cols
    )
    inner_term = of_everyone(jnp.sum(d_act * normed, axis=(1, 2)), "row") / feature_count
    d_inter = (inv_rms * (d_act - normed * inner_term[:, None, None])).astype(jnp.bfloat16)
    back_fold = of_everyone(
        jnp.einsum("bek,bde->bdk", d_inter, embeddings, preferred_element_type=jnp.float32), "row"
    )
    grad_proj = of_everyone(
        jnp.einsum("bde,bdk->ek", emb_float, back_fold, precision=highest), ("batch", "col")
    )
    return (mixed, grad_out, grad_in, grad_bias, grad_proj)


def solution(mesh):
    placed = (
        P("batch", "col", "row"),
        P(),
        P("row", "col"),
        P("col"),
        P(None, "col", "row"),
        P("batch", "col", "row"),
    )
    return jax.shard_map(
        local,
        mesh=mesh,
        in_specs=placed,
        out_specs=(
            P("batch", "col", "row"),
            P("batch", "col", "row"),
            P("row", "col"),
            P("col"),
            P("row", None),
        ),
        check_vma=False,
    )
```

profile of v0, /device:TPU:1, one launch (start us, length us, event | category | flops | bytes accessed | tf_op | source)
XLA Modules:
  0.0 535.5 jit_solution(8240638500809765838)
XLA Ops:
  9.3 4.8 all-to-all-start
  14.4 7.4 %dot_general.47 = bf16[16,128,1024]{2,1,0:T(8,128)(2,1)} reshape(bf16[2048,8,128]{2,1,0:T(8,128)(2,1)} %param.10) | data formatting | bytes 8388608 | tf_op jit(solution)/shard_map/dot_general | solution.py:74
  22.1 3.2 convolution_bitcast_fusion.1
  25.3 4.7 convolution_bitcast_fusion.2
  30.0 11.6 %all-to-all-start.4 = ((f32[16,128,128]{2,1,0:T(8,128)}), f32[16,128,128]{2,1,0:T(8,128)}, u32[]{:S(2)}, u32[]{:S(2)}) async-start(f32[16,128,128]{2,1,0:T(8,128)} %convolution_bitcast_fusion.2), calls=%async_computation.4 | async-start | bytes 2097152 | tf_op jit(solution)/shard_map/all_to_all | solution.py:39
  41.6 172.1 %all-reduce.3.cloned.1.call-done = f32[128,128,32]{1,2,0:T(8,128)} async-done(((f32[128,128,32]{1,2,0:T(8,128)}), f32[128,128,32]{1,2,0:T(8,128)}) %all-reduce.3.cloned.1.call-update) | async-done | bytes 2097168 | tf_op jit(solution)/shard_map/psum | solution.py:91
  217.0 3.3 all-to-all-start.1
  225.1 4.0 all-to-all-start.5
  230.4 3.3 copy.58
  236.1 4.2 all-to-all-start.2
  241.3 5.8 %all-to-all-done.2 = f32[4,128,128]{2,1,0:T(8,128)} async-done(((f32[4,128,128]{2,1,0:T(8,128)}), f32[4,128,128]{2,1,0:T(8,128)}, u32[]{:S(2)}, u32[]{:S(2)}) %all-to-all-start.2) | async-done | bytes 262176 | tf_op jit(solution)/shard_map/all_to_all | solution.py:11
  251.4 95.4 %reduce-scatter.2.cloned.1.call-done = f32[8,4096]{1,0:T(8,128)} async-done(((f32[128,4096]{1,0:T(8,128)}), f32[8,4096]{1,0:T(8,128)}) %reduce-scatter.2.cloned.1.call-update) | async-done | bytes 131088 | tf_op jit(solution)/shard_map/reduce_scatter | solution.py:62
  347.1 23.1 %all_to_all.47 = bf16[16,128,128]{1,2,0:T(8,128)(2,1)S(1)} all-to-all(bf16[16,128,128]{1,2,0:T(8,128)(2,1)S(1)} %broadcast_in_dim.19), channel_id=1, replica_groups=mesh['batch'=4,'row'=4,'col'=16] {'col'}, dimensions={0} | all-to-all | bytes 1048576 | tf_op jit(solution)/shard_map/all_to_all | solution.py:11
  372.9 34.7 %all-gather.5.cloned.1.call-done = f32[128,4096]{1,0:T(8,128)} async-done(((f32[8,4096]{1,0:T(8,128)}), f32[128,4096]{1,0:T(8,128)}) %all-gather.5.cloned.1.call-update) | async-done | bytes 2097168 | tf_op jit(solution)/shard_map/all_gather | solution.py:63
  410.5 3.4 copy.65
  413.9 3.5 multiply_reduce_fusion
  417.3 8.2 %all_to_all.48 = f32[4,1,128]{2,1,0:T(1,128)S(1)} all-to-all(f32[4,1,128]{2,1,0:T(1,128)S(1)} %broadcast_in_dim.21), channel_id=1, replica_groups=mesh['batch'=4,'row'=4,'col'=16] {'row'}, dimensions={0} | all-to-all | bytes 4096 | tf_op jit(solution)/shard_map/all_to_all | solution.py:11
  425.5 3.1 convolution_bitcast_fusion.3
  430.8 3.5 all-to-all-start.7
  436.2 5.1 all-to-all-done.7
  442.6 10.9 %all-to-all-start.8 = ((f32[64,128,32]{1,2,0:T(8,128)}), f32[64,128,32]{1,2,0:T(8,128)S(1)}, u32[]{:S(2)}, u32[]{:S(2)}) async-start(f32[64,128,32]{1,2,0:T(8,128)} %broadcast_in_dim.23), calls=%async_computation.9 | async-start | bytes 2097152 | tf_op jit(solution)/shard_map/all_to_all | solution.py:11
  453.6 33.7 %psum.23 = f32[128]{0:T(128)} all-reduce(f32[128]{0:T(128)S(1)} %get-tuple-element.5), channel_id=1, replica_groups=mesh['batch'=4,'row'=4,'col'=16] {'batch'}, use_global_device_ids=true, to_apply=%region_9.10 | all-reduce | flops 128 | bytes 1024 | tf_op jit(solution)/shard_map/psum | solution.py:119
  497.1 28.8 %all-reduce.5.cloned.1.call-done = f32[4096,128]{1,0:T(8,128)} async-done(((f32[4096,128]{1,0:T(8,128)}), f32[4096,128]{1,0:T(8,128)}) %all-reduce.5.cloned.1.call-update) | async-done | bytes 2097168 | tf_op jit(solution)/shard_map/psum | solution.py:119
  525.9 3.0 copy.87
  (72 shorter events, 40.8 us)
Async XLA Ops:
  7.2 226.5 %copy-start = (bf16[4096,128]{1,0:T(8,128)(2,1)S(1)}, bf16[4096,128]{1,0:T(8,128)(2,1)}, u32[]{:S(2)}) copy-start(bf16[4096,128]{1,0:T(8,128)(2,1)} %param.8) | copy-start | bytes 3145732
  7.2 7.0 %copy-start.7 = (bf16[128,8,128]{2,1,0:T(8,128)(2,1)S(1)}, bf16[128,8,128]{2,1,0:T(8,128)(2,1)}, u32[]{:S(2)}) copy-start(bf16[128,8,128]{2,1,0:T(8,128)(2,1)} %param.11) | copy-start | bytes 786436
  9.3 12.5 %all-to-all-start = ((f32[4,128,8,32]{1,3,2,0:T(8,128)}), f32[4,128,8,32]{1,3,2,0:T(8,128)S(1)}, u32[]{:S(2)}, u32[]{:S(2)}) async-start(f32[4,128,8,32]{1,3,2,0:T(8,128)} %broadcast_in_dim.16), calls=%async_computation | async-start | bytes 1048576 | tf_op jit(solution)/shard_map/all_to_all | solution.py:11
  14.2 199.5 %all-reduce.3.cloned.1.call-start = ((), (), s32[]{:S(2)}) async-start(), calls=%async_computation.10 | async-start | bytes 4194304 | tf_op jit(solution)/shard_map/psum | solution.py:91
  14.4 10.9 %copy-start.4 = (bf16[128,8,128]{0,2,1:T(8,128)(2,1)}, bf16[128,8,128]{0,2,1:T(8,128)(2,1)S(1)}, u32[]{:S(2)}) copy-start(bf16[128,8,128]{0,2,1:T(8,128)(2,1)S(1)} %copy.60) | copy-start | bytes 786436
  14.4 7.7 %copy-start.3 = (bf16[128,8,128]{2,1,0:T(8,128)(2,1)S(1)}, bf16[128,8,128]{2,1,0:T(8,128)(2,1)}, u32[]{:S(2)}) copy-start(bf16[128,8,128]{2,1,0:T(8,128)(2,1)} %param.6) | copy-start | bytes 786436
  30.0 186.4 %all-to-all-start.4 = ((f32[16,128,128]{2,1,0:T(8,128)}), f32[16,128,128]{2,1,0:T(8,128)}, u32[]{:S(2)}, u32[]{:S(2)}) async-start(f32[16,128,128]{2,1,0:T(8,128)} %convolution_bitcast_fusion.2), calls=%async_computation.4 | async-start | bytes 2097152 | tf_op jit(solution)/shard_map/all_to_all | solution.py:39
  213.7 15.5 %copy-start.1 = (f32[128,128,32]{1,2,0:T(8,128)S(1)}, f32[128,128,32]{1,2,0:T(8,128)}, u32[]{:S(2)}) copy-start(f32[128,128,32]{1,2,0:T(8,128)} %all-reduce.3.cloned.1.call-done) | copy-start | bytes 6291460
  217.0 7.4 %all-to-all-start.1 = ((f32[4,1,128]{2,1,0:T(1,128)}), f32[4,1,128]{2,1,0:T(1,128)S(1)}, u32[]{:S(2)}, u32[]{:S(2)}) async-start(f32[4,1,128]{2,1,0:T(1,128)} %broadcast_in_dim.17), calls=%async_computation.1 | async-start | bytes 4096 | tf_op jit(solution)/shard_map/all_to_all | solution.py:11
  225.1 10.3 %all-to-all-start.5 = ((f32[4,128,128]{2,1,0:T(8,128)}), f32[4,128,128]{2,1,0:T(8,128)}, u32[]{:S(2)}, u32[]{:S(2)}) async-start(f32[4,128,128]{2,1,0:T(8,128)} %broadcast_in_dim.20), calls=%async_computation.5 | async-start | bytes 524288 | tf_op jit(solution)/shard_map/all_to_all | solution.py:11
  233.7 15.0 %copy-start.8 = (f32[128]{0:T(128)S(1)}, f32[128]{0:T(128)}, u32[]{:S(2)}) copy-start(f32[128]{0:T(128)} %param.9) | copy-start | bytes 1540
  236.1 10.9 %all-to-all-start.2 = ((f32[4,128,128]{2,1,0:T(8,128)}), f32[4,128,128]{2,1,0:T(8,128)}, u32[]{:S(2)}, u32[]{:S(2)}) async-start(f32[4,128,128]{2,1,0:T(8,128)} %broadcast_in_dim.18), calls=%async_computation.2 | async-start | bytes 524288 | tf_op jit(solution)/shard_map/all_to_all | solution.py:11
  240.3 106.5 %reduce-scatter.2.cloned.1.call-start = ((), (), s32[]{:S(2)}) async-start(), calls=%async_computation.13 | async-start | bytes 2228224 | tf_op jit(solution)/shard_map/reduce_scatter | solution.py:62
  251.4 156.3 %all-gather.5.cloned.1.call-start = ((), (), s32[]{:S(2)}) async-start(), calls=%async_computation.14 | async-start | bytes 2228224 | tf_op jit(solution)/shard_map/all_gather | solution.py:63
  346.9 144.2 %all-gather.3.cloned.1.call-start = ((), (), s32[]{:S(2)}) async-start(), calls=%async_computation.11 | async-start | bytes 3932160 | tf_op jit(solution)/shard_map/all_gather | solution.py:45
  370.2 0.8 copy-start.5
  428.7 5.7 %copy-start.2 = (bf16[128,128,32]{0,2,1:T(8,128)(2,1)S(1)}, bf16[128,128,32]{0,2,1:T(8,128)(2,1)}, u32[]{:S(2)}) copy-start(bf16[128,128,32]{0,2,1:T(8,128)(2,1)} %copy.58) | copy-start | bytes 3145732
  430.8 10.4 %all-to-all-start.7 = ((f32[4,128,8,32]{1,3,2,0:T(8,128)}), f32[4,128,8,32]{1,3,2,0:T(8,128)S(1)}, u32[]{:S(2)}, u32[]{:S(2)}) async-start(f32[4,128,8,32]{1,3,2,0:T(8,128)} %broadcast_in_dim.22), calls=%async_computation.8 | async-start | bytes 1048576 | tf_op jit(solution)/shard_map/all_to_all | solution.py:11
  434.3 91.6 %all-reduce.5.cloned.1.call-start = ((), (), s32[]{:S(2)}) async-start(), calls=%async_computation.12 | async-start | bytes 4194304 | tf_op jit(solution)/shard_map/psum | solution.py:119
  436.1 51.2 %copy-start.6 = (bf16[16,128,128]{1,2,0:T(8,128)(2,1)S(1)}, bf16[16,128,128]{1,2,0:T(8,128)(2,1)}, u32[]{:S(2)}) copy-start(bf16[16,128,128]{1,2,0:T(8,128)(2,1)} %copy-done.5) | copy-start | bytes 1572868
  442.6 53.8 %all-to-all-start.8 = ((f32[64,128,32]{1,2,0:T(8,128)}), f32[64,128,32]{1,2,0:T(8,128)S(1)}, u32[]{:S(2)}, u32[]{:S(2)}) async-start(f32[64,128,32]{1,2,0:T(8,128)} %broadcast_in_dim.23), calls=%async_computation.9 | async-start | bytes 2097152 | tf_op jit(solution)/shard_map/all_to_all | solution.py:11
  491.1 1.6 slice-start
Sparse Core Ops, SparseCore 0:
  25.4 188.1 all-reduce.2
  251.5 95.3 reduce-scatter.1
  349.3 58.3 all-gather.4
  409.3 39.9 all-gather.2
  452.4 73.5 all-reduce.4
where the time goes:
time: 537 us; the launch traced here: 536 us
  waiting for transfers between devices  345 us (64%)
  blocking collectives  65 us (12%)
  starting transfers between devices  42.5 us (8%)
  local copies, waits for them, and re-layouts  31.8 us (6%)
  matrix products  22.6 us (4%)
  other arithmetic  14.9 us (3%)
  between operations  14 us (3%)
    psum x1, waiting for transfers between devices, local(): interact = lax.psum(partial_value, 'col')  172 us
    reduce_scatter x1, waiting for transfers between devices, sum_by_parts(): own = lax.psum_scatter(padded, axis, scatter_dimension=0, tiled=True)  95.4 us
    all_gather x1, waiting for transfers between devices, sum_by_parts(): whole = lax.all_gather(own, axis, axis=0, tiled=True)  34.7 us
    psum x1, blocking collectives, local(): lax.psum((contract_first(activated, d_pre_b), jnp.sum(d_preact, axis=0)),...  33.7 us
    all_to_all x2, blocking collectives, copy_for_each(): lax.all_to_all(jnp.broadcast_to(array[None], (size, *array.shape)), axis,...  31.3 us
    all_to_all x6, starting transfers between devices, copy_for_each(): lax.all_to_all(jnp.broadcast_to(array[None], (size, *array.shape)), axis,...  30.8 us
    psum x1, waiting for transfers between devices, local(): lax.psum((contract_first(activated, d_pre_b), jnp.sum(d_preact, axis=0)),...  28.8 us
    all_to_all x6, waiting for transfers between devices, copy_for_each(): lax.all_to_all(jnp.broadcast_to(array[None], (size, *array.shape)), axis,...  13.6 us
  transfers between devices with their start and end apart: 12, of which 7 were waited for; matrix products, arithmetic and copies ran while one was open for 10% of the time, Pallas kernels for 0%

commit v1 on v0

--- a/solution.py
+++ b/solution.py
@@ -60,7 +60,10 @@
     lines = array.reshape(-1, *array.shape[1:][-1:])
     padded = filled_up(lines, lax.axis_size(axis))
     own = lax.psum_scatter(padded, axis, scatter_dimension=0, tiled=True)
-    whole = lax.all_gather(own, axis, axis=0, tiled=True)
+    whole = jnp.concatenate(
+        lax.all_to_all(jnp.stack([own] * lax.axis_size(axis)), axis, split_axis=0, concat_axis=0),
+        axis=0,
+    )
     return whole[: len(lines)].reshape(array.shape)
 
 

time: 537 us -> 555 us (1.034)
  starting transfers between devices: 42.5 us -> 54.6 us
  local copies, waits for them, and re-layouts: 31.8 us -> 39.7 us
    all_to_all x0 -> x1, waiting for transfers between devices: none -> 56.9 us  [sum_by_parts(): lax.all_to_all(jnp.stack([own] * lax.axis_size(axis)), axis, split_axis=0...]
    all_gather x1 -> x0, waiting for transfers between devices: 34.7 us -> none  [sum_by_parts(): whole = lax.all_gather(own, axis, axis=0, tiled=True)]
    reduce_scatter x1, waiting for transfers between devices: 95.4 us -> 79.8 us  [sum_by_parts(): own = lax.psum_scatter(padded, axis, scatter_dimension=0, tiled=True)]
    another operation x0 -> x3, local copies, waits for them, and re-layouts: none -> 15.1 us  [the longest x2 12.7 us: local(): sum_by_parts(contract_last(d_pre_b, w_in), 'col')]
    psum x1, waiting for transfers between devices: 28.8 us -> 21.5 us  [local(): lax.psum((contract_first(activated, d_pre_b), jnp.sum(d_preact, axis=0)),...]
    all_to_all x6, starting transfers between devices: 30.8 us -> 36.8 us  [copy_for_each(): lax.all_to_all(jnp.broadcast_to(array[None], (size, *array.shape)), axis,...]
    all_to_all x0 -> x1, starting transfers between devices: none -> 5.92 us  [sum_by_parts(): lax.all_to_all(jnp.stack([own] * lax.axis_size(axis)), axis, split_axis=0...]
    all_to_all x2, blocking collectives: 31.3 us -> 25.7 us  [copy_for_each(): lax.all_to_all(jnp.broadcast_to(array[None], (size, *array.shape)), axis,...]
  transfers between devices with their start and end apart: 12 -> 12, of which waited for: 7 -> 7; matrix products, arithmetic and copies ran while one was open for 10% -> 11% of each run, Pallas kernels for 0% -> 0%
where the time goes in v1:
time: 555 us; the launch traced here: 554 us
  waiting for transfers between devices  344 us (62%)
  blocking collectives  63.9 us (12%)
  starting transfers between devices  54.6 us (10%)
  local copies, waits for them, and re-layouts  39.7 us (7%)
  matrix products  22.5 us (4%)
  other arithmetic  15.1 us (3%)
  between operations  14 us (3%)
    psum x1, waiting for transfers between devices, local(): interact = lax.psum(partial_value, 'col')  172 us
    reduce_scatter x1, waiting for transfers between devices, sum_by_parts(): own = lax.psum_scatter(padded, axis, scatter_dimension=0, tiled=True)  79.8 us
    all_to_all x1, waiting for transfers between devices, sum_by_parts(): lax.all_to_all(jnp.stack([own] * lax.axis_size(axis)), axis, split_axis=0...  56.9 us
    psum x1, blocking collectives, local(): lax.psum((contract_first(activated, d_pre_b), jnp.sum(d_preact, axis=0)),...  38.3 us
    all_to_all x6, starting transfers between devices, copy_for_each(): lax.all_to_all(jnp.broadcast_to(array[None], (size, *array.shape)), axis,...  36.8 us
    all_to_all x2, blocking collectives, copy_for_each(): lax.all_to_all(jnp.broadcast_to(array[None], (size, *array.shape)), axis,...  25.7 us
    psum x1, waiting for transfers between devices, local(): lax.psum((contract_first(activated, d_pre_b), jnp.sum(d_preact, axis=0)),...  21.5 us
    all_to_all x6, waiting for transfers between devices, copy_for_each(): lax.all_to_all(jnp.broadcast_to(array[None], (size, *array.shape)), axis,...  13.4 us
  transfers between devices with their start and end apart: 12, of which 7 were waited for; matrix products, arithmetic and copies ran while one was open for 11% of the time, Pallas kernels for 0%

profile of v1, /device:TPU:1, one launch (start us, length us, event | category | flops | bytes accessed | tf_op | source)
XLA Modules:
  0.0 553.5 jit_solution(11179634422010670983)
XLA Ops:
  9.3 4.8 all-to-all-start
  14.4 7.4 %dot_general.47 = bf16[16,128,1024]{2,1,0:T(8,128)(2,1)} reshape(bf16[2048,8,128]{2,1,0:T(8,128)(2,1)} %param.10) | data formatting | bytes 8388608 | tf_op jit(solution)/shard_map/dot_general | solution.py:77
  22.1 3.2 convolution_bitcast_fusion.1
  25.3 4.7 convolution_bitcast_fusion.2
  30.0 11.6 %all-to-all-start.4 = ((f32[16,128,128]{2,1,0:T(8,128)}), f32[16,128,128]{2,1,0:T(8,128)}, u32[]{:S(2)}, u32[]{:S(2)}) async-start(f32[16,128,128]{2,1,0:T(8,128)} %convolution_bitcast_fusion.2), calls=%async_computation.4 | async-start | bytes 2097152 | tf_op jit(solution)/shard_map/all_to_all | solution.py:39
  41.6 172.1 %all-reduce.3.cloned.1.call-done = f32[128,128,32]{1,2,0:T(8,128)} async-done(((f32[128,128,32]{1,2,0:T(8,128)}), f32[128,128,32]{1,2,0:T(8,128)}) %all-reduce.3.cloned.1.call-update) | async-done | bytes 2097168 | tf_op jit(solution)/shard_map/psum | solution.py:94
  217.0 3.3 all-to-all-start.1
  225.1 4.0 all-to-all-start.5
  230.4 3.2 copy.54
  236.0 4.2 all-to-all-start.2
  241.2 5.7 %all-to-all-done.2 = f32[4,128,128]{2,1,0:T(8,128)} async-done(((f32[4,128,128]{2,1,0:T(8,128)}), f32[4,128,128]{2,1,0:T(8,128)}, u32[]{:S(2)}, u32[]{:S(2)}) %all-to-all-start.2) | async-done | bytes 262176 | tf_op jit(solution)/shard_map/all_to_all | solution.py:11
  251.4 17.9 %all_to_all.52 = bf16[16,128,128]{1,2,0:T(8,128)(2,1)} all-to-all(bf16[16,128,128]{1,2,0:T(8,128)(2,1)S(1)} %broadcast_in_dim.19), channel_id=1, replica_groups=mesh['batch'=4,'row'=4,'col'=16] {'col'}, dimensions={0} | all-to-all | bytes 1048576 | tf_op jit(solution)/shard_map/all_to_all | solution.py:11
  269.3 79.8 %reduce-scatter.2.cloned.1.call-done = f32[8,4096]{1,0:T(8,128)} async-done(((f32[128,4096]{1,0:T(8,128)}), f32[8,4096]{1,0:T(8,128)}) %reduce-scatter.2.cloned.1.call-update) | async-done | bytes 131088 | tf_op jit(solution)/shard_map/reduce_scatter | solution.py:62
  351.5 5.9 %all-to-all-start.6 = ((f32[16,8,4096]{2,1,0:T(8,128)}), f32[16,8,4096]{2,1,0:T(8,128)}, u32[]{:S(2)}, u32[]{:S(2)}) async-start(f32[16,8,4096]{2,1,0:T(8,128)} %stack.2), calls=%async_computation.7 | async-start | bytes 4194304 | tf_op jit(solution)/shard_map/all_to_all | solution.py:64
  359.5 56.9 %all-to-all-done.6 = f32[16,8,4096]{2,1,0:T(8,128)} async-done(((f32[16,8,4096]{2,1,0:T(8,128)}), f32[16,8,4096]{2,1,0:T(8,128)}, u32[]{:S(2)}, u32[]{:S(2)}) %all-to-all-start.6) | async-done | bytes 2097184 | tf_op jit(solution)/shard_map/all_to_all | solution.py:64
  416.4 6.4 %reshape_reshape.3 = f32[128,128,32]{2,1,0:T(8,128)} reshape(f32[16,8,4096]{2,1,0:T(8,128)} %all-to-all-done.6) | data formatting | bytes 4194304 | tf_op jit(solution)/shard_map/reshape;reshape | solution.py:125
  422.8 6.2 %copy.60 = f32[128,128,32]{1,2,0:T(8,128)} copy(f32[128,128,32]{2,1,0:T(8,128)} %reshape_reshape.3) | data formatting | bytes 4194304 | tf_op jit(solution)/shard_map/reshape;reshape | solution.py:125
  429.1 3.5 multiply_reduce_fusion
  432.6 7.8 %all_to_all.53 = f32[4,1,128]{2,1,0:T(1,128)S(1)} all-to-all(f32[4,1,128]{2,1,0:T(1,128)S(1)} %broadcast_in_dim.21), channel_id=1, replica_groups=mesh['batch'=4,'row'=4,'col'=16] {'row'}, dimensions={0} | all-to-all | bytes 4096 | tf_op jit(solution)/shard_map/all_to_all | solution.py:11
  445.6 3.5 all-to-all-start.8
  451.1 4.9 all-to-all-done.8
  457.4 17.0 %all-to-all-start.9 = ((f32[64,128,32]{1,2,0:T(8,128)}), f32[64,128,32]{1,2,0:T(8,128)S(1)}, u32[]{:S(2)}, u32[]{:S(2)}) async-start(f32[64,128,32]{1,2,0:T(8,128)} %broadcast_in_dim.23), calls=%async_computation.10 | async-start | bytes 2097152 | tf_op jit(solution)/shard_map/all_to_all | solution.py:11
  474.4 38.3 %psum.23 = f32[128]{0:T(128)} all-reduce(f32[128]{0:T(128)S(1)} %get-tuple-element.5), channel_id=1, replica_groups=mesh['batch'=4,'row'=4,'col'=16] {'batch'}, use_global_device_ids=true, to_apply=%region_9.10 | all-reduce | flops 128 | bytes 1024 | tf_op jit(solution)/shard_map/psum | solution.py:122
  522.4 21.5 %all-reduce.5.cloned.1.call-done = f32[4096,128]{1,0:T(8,128)} async-done(((f32[4096,128]{1,0:T(8,128)}), f32[4096,128]{1,0:T(8,128)}) %all-reduce.5.cloned.1.call-update) | async-done | bytes 2097168 | tf_op jit(solution)/shard_map/psum | solution.py:122
  (70 shorter events, 45.9 us)
Async XLA Ops:
  7.2 226.4 %copy-start = (bf16[4096,128]{1,0:T(8,128)(2,1)S(1)}, bf16[4096,128]{1,0:T(8,128)(2,1)}, u32[]{:S(2)}) copy-start(bf16[4096,128]{1,0:T(8,128)(2,1)} %param.8) | copy-start | bytes 3145732
  7.2 7.0 %copy-start.6 = (bf16[128,8,128]{2,1,0:T(8,128)(2,1)S(1)}, bf16[128,8,128]{2,1,0:T(8,128)(2,1)}, u32[]{:S(2)}) copy-start(bf16[128,8,128]{2,1,0:T(8,128)(2,1)} %param.11) | copy-start | bytes 786436
  9.3 12.5 %all-to-all-start = ((f32[4,128,8,32]{1,3,2,0:T(8,128)}), f32[4,128,8,32]{1,3,2,0:T(8,128)S(1)}, u32[]{:S(2)}, u32[]{:S(2)}) async-start(f32[4,128,8,32]{1,3,2,0:T(8,128)} %broadcast_in_dim.16), calls=%async_computation | async-start | bytes 1048576 | tf_op jit(solution)/shard_map/all_to_all | solution.py:11
  14.2 199.5 %all-reduce.3.cloned.1.call-start = ((), (), s32[]{:S(2)}) async-start(), calls=%async_computation.11 | async-start | bytes 4194304 | tf_op jit(solution)/shard_map/psum | solution.py:94
  14.4 10.9 %copy-start.4 = (bf16[128,8,128]{0,2,1:T(8,128)(2,1)}, bf16[128,8,128]{0,2,1:T(8,128)(2,1)S(1)}, u32[]{:S(2)}) copy-start(bf16[128,8,128]{0,2,1:T(8,128)(2,1)S(1)} %copy.56) | copy-start | bytes 786436
  14.4 7.7 %copy-start.3 = (bf16[128,8,128]{2,1,0:T(8,128)(2,1)S(1)}, bf16[128,8,128]{2,1,0:T(8,128)(2,1)}, u32[]{:S(2)}) copy-start(bf16[128,8,128]{2,1,0:T(8,128)(2,1)} %param.6) | copy-start | bytes 786436
  30.0 186.4 %all-to-all-start.4 = ((f32[16,128,128]{2,1,0:T(8,128)}), f32[16,128,128]{2,1,0:T(8,128)}, u32[]{:S(2)}, u32[]{:S(2)}) async-start(f32[16,128,128]{2,1,0:T(8,128)} %convolution_bitcast_fusion.2), calls=%async_computation.4 | async-start | bytes 2097152 | tf_op jit(solution)/shard_map/all_to_all | solution.py:39
  213.7 15.5 %copy-start.1 = (f32[128,128,32]{1,2,0:T(8,128)S(1)}, f32[128,128,32]{1,2,0:T(8,128)}, u32[]{:S(2)}) copy-start(f32[128,128,32]{1,2,0:T(8,128)} %all-reduce.3.cloned.1.call-done) | copy-start | bytes 6291460
  217.0 7.4 %all-to-all-start.1 = ((f32[4,1,128]{2,1,0:T(1,128)}), f32[4,1,128]{2,1,0:T(1,128)S(1)}, u32[]{:S(2)}, u32[]{:S(2)}) async-start(f32[4,1,128]{2,1,0:T(1,128)} %broadcast_in_dim.17), calls=%async_computation.1 | async-start | bytes 4096 | tf_op jit(solution)/shard_map/all_to_all | solution.py:11
  225.1 10.2 %all-to-all-start.5 = ((f32[4,128,128]{2,1,0:T(8,128)}), f32[4,128,128]{2,1,0:T(8,128)}, u32[]{:S(2)}, u32[]{:S(2)}) async-start(f32[4,128,128]{2,1,0:T(8,128)} %broadcast_in_dim.20), calls=%async_computation.5 | async-start | bytes 524288 | tf_op jit(solution)/shard_map/all_to_all | solution.py:11
  233.6 14.9 %copy-start.7 = (f32[128]{0:T(128)S(1)}, f32[128]{0:T(128)}, u32[]{:S(2)}) copy-start(f32[128]{0:T(128)} %param.9) | copy-start | bytes 1540
  236.0 10.9 %all-to-all-start.2 = ((f32[4,128,128]{2,1,0:T(8,128)}), f32[4,128,128]{2,1,0:T(8,128)}, u32[]{:S(2)}, u32[]{:S(2)}) async-start(f32[4,128,128]{2,1,0:T(8,128)} %broadcast_in_dim.18), calls=%async_computation.2 | async-start | bytes 524288 | tf_op jit(solution)/shard_map/all_to_all | solution.py:11
  240.2 108.8 %reduce-scatter.2.cloned.1.call-start = ((), (), s32[]{:S(2)}) async-start(), calls=%async_computation.14 | async-start | bytes 2228224 | tf_op jit(solution)/shard_map/reduce_scatter | solution.py:62
  351.5 65.0 %all-to-all-start.6 = ((f32[16,8,4096]{2,1,0:T(8,128)}), f32[16,8,4096]{2,1,0:T(8,128)}, u32[]{:S(2)}, u32[]{:S(2)}) async-start(f32[16,8,4096]{2,1,0:T(8,128)} %stack.2), calls=%async_computation.7 | async-start | bytes 4194304 | tf_op jit(solution)/shard_map/all_to_all | solution.py:64
  357.4 159.0 %all-gather.2.cloned.1.call-start = ((), (), s32[]{:S(2)}) async-start(), calls=%async_computation.12 | async-start | bytes 3932160 | tf_op jit(solution)/shard_map/all_gather | solution.py:45
  443.5 5.9 %copy-start.2 = (bf16[128,128,32]{0,2,1:T(8,128)(2,1)S(1)}, bf16[128,128,32]{0,2,1:T(8,128)(2,1)}, u32[]{:S(2)}) copy-start(bf16[128,128,32]{0,2,1:T(8,128)(2,1)} %copy.54) | copy-start | bytes 3145732
  445.6 10.4 %all-to-all-start.8 = ((f32[4,128,8,32]{1,3,2,0:T(8,128)}), f32[4,128,8,32]{1,3,2,0:T(8,128)S(1)}, u32[]{:S(2)}, u32[]{:S(2)}) async-start(f32[4,128,8,32]{1,3,2,0:T(8,128)} %broadcast_in_dim.22), calls=%async_computation.9 | async-start | bytes 1048576 | tf_op jit(solution)/shard_map/all_to_all | solution.py:11
  449.1 94.8 %all-reduce.5.cloned.1.call-start = ((), (), s32[]{:S(2)}) async-start(), calls=%async_computation.13 | async-start | bytes 4194304 | tf_op jit(solution)/shard_map/psum | solution.py:122
  451.1 61.6 %copy-start.5 = (bf16[16,128,128]{1,2,0:T(8,128)(2,1)S(1)}, bf16[16,128,128]{1,2,0:T(8,128)(2,1)}, u32[]{:S(2)}) copy-start(bf16[16,128,128]{1,2,0:T(8,128)(2,1)} %all_to_all.52) | copy-start | bytes 1572868
  457.4 64.3 %all-to-all-start.9 = ((f32[64,128,32]{1,2,0:T(8,128)}), f32[64,128,32]{1,2,0:T(8,128)S(1)}, u32[]{:S(2)}, u32[]{:S(2)}) async-start(f32[64,128,32]{1,2,0:T(8,128)} %broadcast_in_dim.23), calls=%async_computation.10 | async-start | bytes 2097152 | tf_op jit(solution)/shard_map/all_to_all | solution.py:11
  516.4 1.6 slice-start
Sparse Core Ops, SparseCore 0:
  25.4 188.1 all-reduce.2
  251.3 97.6 reduce-scatter.1
  360.0 69.1 all-gather.1
  452.9 91.0 all-reduce.4
